TPU v7x, 256 devices: a whole 4x4x8 slice. The times are simulated.
256 devices in a mesh: dp: 8 (over x, y_hi), row: 4 (over y_lo, core), col: 8 (over z).
Axes of the slice: x: 4, y: 4 (y_hi: 2, y_lo: 2; y = y_hi * 2 + y_lo), z: 8, core: 2. Of those that a mesh axis runs over, the one named last changes fastest.
Arguments:
- teacher_in: bfloat16 [8, 128, 256, 384], P('dp', 'row', 'col'), may hold values from -6 to 6
- student_in: bfloat16 [8, 128, 256, 384], P('dp', 'row', 'col'), may hold values from -6 to 6
- cotangent: bfloat16 [8, 128, 256, 384], P('dp', 'row', 'col'), may hold values from -6 to 6
- kernels: bfloat16 [2, 49, 384], replicated, may hold values from -0.875 to 0.875
- norm_gains: bfloat16 [2, 2, 384], replicated, may hold values from 0.25 to 1.75
- biases: bfloat16 [2, 3, 384], replicated, may hold values from -3 to 3
- weight_in: bfloat16 [2, 384, 1536], P(None, None, 'dp'), may hold values from -0.3125 to 0.3125
- bias_in: bfloat16 [2, 1536], P(None, 'dp'), may hold values from -3 to 3
- weight_out: bfloat16 [2, 1536, 384], P(None, 'dp'), may hold values from -0.15625 to 0.15625
Outputs:
- teacher_out: float32 [8, 128, 256, 384], P('dp', 'row', 'col')
- student_out: float32 [8, 128, 256, 384], P('dp', 'row', 'col')
- input_grad: float32 [8, 128, 256, 384], P('dp', 'row', 'col')
- grad_weight_in: float32 [384, 1536], P(None, 'dp')
- grad_bias_in: float32 [1536], P('dp')
- grad_weight_out: float32 [1536, 384], P('dp')
- grad_kernel: float32 [49, 384], replicated
- grad_gains: float32 [2, 384], replicated
- grad_biases: float32 [3, 384], replicated
All inputs are finite; a program needn't handle non-finite values.
Results may differ from a plain program's by a relative error of at most 0.0057.
Values may be sent and summed in bfloat16 or wider, within the bound.
No kernel may reach another device: no remote copies, remote signals or barrier semaphores. Data moves between devices by JAX's collectives and lax.ppermute only.
A program may use at most 128 MiB of HBM per device.

v0:
```python
import jax
import jax.numpy as jnp
from jax import lax
from jax.sharding import PartitionSpec as P

KERNEL = 7
EPSILON = 1e-06
ROOT_HALF = 0.7071067811865476
INV_ROOT_TWO_PI = 0.3989422804014327


def with_halo(value, sides, width):
    for axis, dim in sides:
        peers, length = (lax.axis_size(axis), value.shape[dim])
        up = [(i, (i + 1) % peers) for i in range(peers - 1)]
        down = [(j, i) for i, j in up]
        last = lax.slice_in_dim(value, length - width, length, axis=dim)
        leading = lax.slice_in_dim(value, 0, width, axis=dim)
        before = lax.ppermute(last, axis, up)
        after = lax.ppermute(leading, axis, down)
        value = jnp.concatenate([before, value, after], axis=dim)
    return value


def gelu_value(before):
    return before * 0.5 * (1.0 + lax.erf(before * ROOT_HALF))


def gelu_slope(before):
    return 0.5 * (1.0 + lax.erf(before * ROOT_HALF)) + before * INV_ROOT_TWO_PI * jnp.exp(
        -0.5 * before * before
    )


def depthwise(padded, kernel, height, breadth):
    running = jnp.zeros((padded.shape[0], height, breadth, padded.shape[3]), jnp.float32)
    for position in range(KERNEL * KERNEL):
        vertical = position // KERNEL
        lateral = position % KERNEL
        window = padded[:, vertical : vertical + height, lateral : lateral + breadth, :]
        running = running + window.astype(jnp.float32) * kernel[position].astype(jnp.float32)
    return running


def forward(padded, inputs, kernel, norm_gains, biases, weight_in, bias_in, weight_out):
    height, breadth, channels = (inputs.shape[1], inputs.shape[2], inputs.shape[3])
    convolved = depthwise(padded, kernel, height, breadth) + biases[0].astype(jnp.float32)
    centered = convolved - jnp.mean(convolved, axis=-1, keepdims=True)
    inverse = lax.rsqrt(jnp.mean(centered * centered, axis=-1, keepdims=True) + EPSILON)
    scaled = centered * inverse
    normed = (scaled * norm_gains[0].astype(jnp.float32) + biases[1].astype(jnp.float32)).astype(
        jnp.bfloat16
    )
    normed = normed.reshape(-1, channels)
    before = jnp.dot(normed, weight_in, preferred_element_type=jnp.float32) + bias_in.astype(
        jnp.float32
    )
    hidden = gelu_value(before).astype(jnp.bfloat16)
    branch = jnp.dot(hidden, weight_out, preferred_element_type=jnp.float32) + biases[2].astype(
        jnp.float32
    )
    output = inputs.astype(jnp.float32) + norm_gains[1].astype(jnp.float32) * branch.reshape(
        inputs.shape
    )
    return (output, (scaled, inverse, normed, before, hidden, branch))


def backward(cotangent, padded, stored, norm_gains, weight_in, weight_out):
    scaled, inverse, normed, before, hidden, branch = stored
    height, breadth, channels = (cotangent.shape[1], cotangent.shape[2], cotangent.shape[3])
    flat_grad = cotangent.astype(jnp.float32).reshape(-1, channels)
    grad_gamma = jnp.sum(flat_grad * branch, axis=0)
    branch_grad = (flat_grad * norm_gains[1].astype(jnp.float32)).astype(jnp.bfloat16)
    branch_grad = lax.optimization_barrier(branch_grad)
    grad_out_bias = jnp.sum(branch_grad.astype(jnp.float32), axis=0)
    grad_weight_out = jnp.dot(hidden.T, branch_grad, preferred_element_type=jnp.float32)
    hidden_grad = jnp.dot(branch_grad, weight_out.T, preferred_element_type=jnp.float32)
    before_grad = (hidden_grad * gelu_slope(before)).astype(jnp.bfloat16)
    before_grad = lax.optimization_barrier(before_grad)
    grad_bias_in = jnp.sum(before_grad.astype(jnp.float32), axis=0)
    grad_weight_in = jnp.dot(normed.T, before_grad, preferred_element_type=jnp.float32)
    normed_grad = jnp.dot(before_grad, weight_in.T, preferred_element_type=jnp.float32).reshape(
        scaled.shape
    )
    grad_norm_gain = jnp.sum(normed_grad * scaled, axis=(0, 1, 2))
    grad_norm_bias = jnp.sum(normed_grad, axis=(0, 1, 2))
    scaled_grad = normed_grad * norm_gains[0].astype(jnp.float32)
    conv_grad = inverse * (
        scaled_grad
        - jnp.mean(scaled_grad, axis=-1, keepdims=True)
        - scaled * jnp.mean(scaled_grad * scaled, axis=-1, keepdims=True)
    )
    conv_grad = lax.optimization_barrier(conv_grad.astype(jnp.bfloat16))
    conv_wide = conv_grad.astype(jnp.float32)
    grad_conv_bias = jnp.sum(conv_wide, axis=(0, 1, 2))
    tap_sums = []
    for position in range(KERNEL * KERNEL):
        vertical = position // KERNEL
        lateral = position % KERNEL
        window = padded[:, vertical : vertical + height, lateral : lateral + breadth, :].astype(
            jnp.float32
        )
        tap_sums.append(jnp.sum(window * conv_wide, axis=(0, 1, 2)))
    grad_kernel = jnp.stack(tap_sums)
    large_grads = (grad_weight_in, grad_bias_in, grad_weight_out)
    minor_grads = (
        grad_kernel,
        jnp.stack([grad_norm_gain, grad_gamma]),
        jnp.stack([grad_conv_bias, grad_norm_bias, grad_out_bias]),
    )
    return (conv_grad, large_grads, minor_grads)


def input_gradient(cotangent, padded_grad, kernel):
    height, breadth = (cotangent.shape[1], cotangent.shape[2])
    flipped = depthwise(padded_grad, kernel[::-1], height, breadth)
    return cotangent.astype(jnp.float32) + flipped


def on_device(
    teacher_in, student_in, cotangent, kernels, norm_gains, biases, weight_in, bias_in, weight_out
):
    margin = KERNEL // 2
    full_in, full_bias, full_out = (
        lax.all_gather(weight_in, "dp", axis=2, tiled=True),
        lax.all_gather(bias_in, "dp", axis=1, tiled=True),
        lax.all_gather(weight_out, "dp", axis=1, tiled=True),
    )
    teacher_pad = with_halo(teacher_in, (("row", 1), ("col", 2)), margin)
    student_pad = with_halo(student_in, (("row", 1), ("col", 2)), margin)
    teacher_res, unused = forward(
        teacher_pad,
        teacher_in,
        kernels[0],
        norm_gains[0],
        biases[0],
        full_in[0],
        full_bias[0],
        full_out[0],
    )
    student_res, stored = forward(
        student_pad,
        student_in,
        kernels[1],
        norm_gains[1],
        biases[1],
        full_in[1],
        full_bias[1],
        full_out[1],
    )
    conv_grad, large_grads, minor_grads = backward(
        cotangent, student_pad, stored, norm_gains[1], full_in[1], full_out[1]
    )
    grad_pad = with_halo(conv_grad, (("row", 1), ("col", 2)), margin)
    in_grad = input_gradient(cotangent, grad_pad, kernels[1])
    minor_sums = lax.psum((minor_grads[0], minor_grads[1], minor_grads[2]), ("dp", "row", "col"))
    owned = (
        lax.psum_scatter(large_grads[0], "dp", scatter_dimension=1, tiled=True),
        lax.psum_scatter(large_grads[1], "dp", scatter_dimension=0, tiled=True),
        lax.psum_scatter(large_grads[2], "dp", scatter_dimension=0, tiled=True),
    )
    shares = lax.psum((owned[0], owned[1], owned[2]), ("row", "col"))
    tokens = (
        teacher_in.shape[0]
        * teacher_in.shape[1]
        * teacher_in.shape[2]
        * lax.axis_size("dp")
        * lax.axis_size("row")
        * lax.axis_size("col")
    )
    factor = float(tokens) ** (-0.5)
    return (
        teacher_res,
        student_res,
        in_grad,
        shares[0] * factor,
        shares[1] * factor,
        shares[2] * factor,
        minor_sums[0] * factor,
        minor_sums[1] * factor,
        minor_sums[2] * factor,
    )


def solution(mesh):
    placed = (
        P("dp", "row", "col", None),
        P("dp", "row", "col", None),
        P("dp", "row", "col", None),
        P(),
        P(),
        P(),
        P(None, None, "dp"),
        P(None, "dp"),
        P(None, "dp", None),
    )
    return jax.shard_map(
        on_device,
        mesh=mesh,
        in_specs=placed,
        out_specs=(
            P("dp", "row", "col", None),
            P("dp", "row", "col", None),
            P("dp", "row", "col", None),
            P(None, "dp"),
            P("dp"),
            P("dp", None),
            P(),
            P(),
            P(),
        ),
        check_vma=False,
    )
```

profile of v0, /device:TPU:1, one launch (start us, length us, event | category | flops | bytes accessed | tf_op | source)
XLA Modules:
  0.0 829.3 jit_solution(6039890744320597389)
XLA Ops:
  8.9 4.6 collective-permute-start
  13.5 1.9 collective-permute-start.1
  16.4 3.6 collective-permute-start.4
  20.0 1.9 collective-permute-start.5
  26.0 1.5 convert_reduce_fusion.55
  27.7 1.4 convert_reduce_fusion.3
  29.1 1.4 convert_reduce_fusion.56
  30.5 19.7 %all-gather = bf16[8,192,2]{1,2,0:T(2,128)(2,1)S(1)} all-gather(bf16[1,192,2]{1,2,0:T(2,128)(2,1)} %bitcast.59), channel_id=1, replica_groups=mesh['dp'=8,'row'=4,'col'=8] {'dp'}, dimensions={0}, use_global_device_ids=true | all-gather | bytes 6912 | tf_op jit(solution)/shard_map/all_gather | solution.py:126
  52.3 3.5 collective-permute-start.2
  55.8 1.3 collective-permute-start.3
  57.7 4.2 collective-permute-start.6
  62.0 1.5 collective-permute-start.7
  63.5 15.8 %fusion.250 = (f32[32,32]{1,0:T(8,128)S(1)}, f32[1,32,32,384]{3,2,1,0:T(8,128)S(1)}) fusion(f32[384]{0:T(512)S(1)} %get-tuple-element.174, f32[384]{0:T(512)S(1)} %get-tuple-element.117, bf16[1,38,3,384]{3,2,1,0:T(4,128)(2,1)S(1)} %collective-permute-done.3, bf16[1,38,32,384]{3,2,1,0:T(8,128)(2,1)S(1)} %get-tuple-element.218, ...), kind=kLoop, calls=%fused_computation.649 | loop fusion | flops 107740160 | bytes 8267776 | tf_op jit(solution)/shard_map/reduce_sum | solution.py:48
  80.0 16.4 %fusion.248 = (f32[32,32]{1,0:T(8,128)S(1)}, f32[1,32,32,384]{3,2,1,0:T(8,128)S(1)}) fusion(f32[384]{0:T(512)S(1)} %get-tuple-element.171, f32[384]{0:T(512)S(1)} %get-tuple-element.146, bf16[1,38,3,384]{3,2,1,0:T(4,128)(2,1)S(1)} %collective-permute-done.7, bf16[1,38,32,384]{3,2,1,0:T(8,128)(2,1)S(1)} %get-tuple-element.214, ...), kind=kLoop, calls=%fused_computation.648 | loop fusion | flops 107740160 | bytes 8267776 | tf_op jit(solution)/shard_map/reduce_sum | solution.py:48
  96.9 1.5 add_convert_fusion
  98.4 6.7 multiply_convert_fusion
  105.1 33.4 %all-gather.6.cloned.1.call-done = bf16[2,1536,384]{2,1,0:T(8,128)(2,1)} async-done(((bf16[2,192,384]{2,1,0:T(8,128)(2,1)}), bf16[2,1536,384]{2,1,0:T(8,128)(2,1)}) %all-gather.6.cloned.1.call-update) | async-done | bytes 2359312 | tf_op jit(solution)/shard_map/all_gather | solution.py:127
  138.5 5.4 fusion.153
  143.9 4.3 fusion.4
  148.2 1.9 fusion.247
  150.1 1.1 copy-done.6
  152.0 2.1 multiply_convert_fusion.2
  155.3 2.6 fusion.146
  158.0 3.2 fusion.150
  161.4 2.6 fusion.147
  164.1 3.1 fusion.151
  167.4 3.6 fusion.149
  171.1 4.4 stack.220
  175.5 5.2 fusion.258
  181.8 5.1 fusion.257
  189.1 4.3 collective-permute-start.8
  193.5 2.1 collective-permute-start.9
  195.5 2.4 convert_reduce_fusion.1
  197.9 19.3 %all-reduce = f32[1536]{0:T(1024)S(1)} all-reduce(f32[1536]{0:T(1024)S(1)} %convert_reduce_fusion.1), channel_id=3, replica_groups=mesh['dp'=8,'row'=4,'col'=8] {'dp'}, use_global_device_ids=true, to_apply=%region_9.0.clone | all-reduce | flops 1536 | bytes 12288
  217.3 54.5 %psum.43 = f32[192]{0:T(256)S(1)} all-reduce(f32[192]{0:T(256)S(1)} %dynamic-slice.1), channel_id=1, replica_groups=mesh['dp'=8,'row'=4,'col'=8] {'row','col'}, use_global_device_ids=true, to_apply=%region_10.0 | all-reduce | flops 192 | bytes 1536 | tf_op jit(solution)/shard_map/psum | solution.py:162
  271.8 77.7 %all-reduce.1 = (f32[2,384]{1,0:T(2,128)S(1)}, f32[3,384]{1,0:T(4,128)S(1)}) all-reduce(f32[2,384]{1,0:T(2,128)S(1)} %pad_maximum_fusion.11, f32[3,384]{1,0:T(4,128)S(1)} %pad_maximum_fusion.10), channel_id=1, replica_groups=mesh['dp'=8,'row'=4,'col'=8] {'dp','row','col'}, use_global_device_ids=true, to_apply=%region_65.0 | all-reduce | flops 1920 | bytes 15360 | tf_op jit(solution)/shard_map/psum | solution.py:156
  350.7 6.3 convolution_add_fusion.1
  357.0 2.8 convert_add_fusion.1
  360.5 2.3 collective-permute-start.10
  362.8 1.3 collective-permute-start.11
  364.1 56.6 %all-reduce.6.cloned.1.call-done = f32[49,384]{1,0:T(8,128)} async-done(((f32[49,384]{1,0:T(8,128)}), f32[49,384]{1,0:T(8,128)}) %all-reduce.6.cloned.1.call-update) | async-done | bytes 75280 | tf_op jit(solution)/shard_map/psum | solution.py:156
  420.7 1.5 broadcast_multiply_fusion.2
  423.0 79.1 %reduce-scatter.5.cloned.1.call-done = f32[192,384]{1,0:T(8,128)} async-done(((f32[1536,384]{1,0:T(8,128)}), f32[192,384]{1,0:T(8,128)}) %reduce-scatter.5.cloned.1.call-update) | async-done | bytes 294928 | tf_op jit(solution)/shard_map/reduce_scatter | solution.py:160
  502.1 85.7 %reduce-scatter.3.cloned.1.call-done = f32[384,192]{0,1:T(8,128)} async-done(((f32[384,1536]{0,1:T(8,128)}), f32[384,192]{0,1:T(8,128)}) %reduce-scatter.3.cloned.1.call-update) | async-done | bytes 294928 | tf_op jit(solution)/shard_map/reduce_scatter | solution.py:158
  587.9 17.0 %convert_add_fusion.2 = f32[1,32,32,384]{3,2,1,0:T(8,128)} fusion(bf16[1,32,32,384]{3,2,1,0:T(8,128)(2,1)} %param.11, bf16[1,32,32,384]{3,2,1,0:T(8,128)(2,1)S(1)} %multiply_convert_fusion.2, bf16[1,3,32,384]{3,2,1,0:T(8,128)(2,1)S(1)} %collective-permute-done.9, bf16[1,3,32,384]{3,2,1,0:T(8,128)(2,1)S(1)} %collective-permute-done.8, ...), kind=kLoop, calls=%fused_computation.342 | loop fusion | flops 60555264 | bytes 36398592 | tf_op jit(solution)/shard_map/add | solution.py:117
  604.9 214.2 %all-reduce.8.cloned.1.call-done = (f32[384,192]{0,1:T(8,128)}, f32[192,384]{1,0:T(8,128)}) async-done(((f32[384,192]{0,1:T(8,128)}, f32[192,384]{1,0:T(8,128)}), (f32[384,192]{0,1:T(8,128)}, f32[192,384]{1,0:T(8,128)})) %all-reduce.8.cloned.1.call-update) | async-done | bytes 589840 | tf_op jit(solution)/shard_map/psum | solution.py:162
  819.0 1.7 broadcast_multiply_fusion
  820.7 1.7 broadcast_multiply_fusion.1
  (248 shorter events, 17.5 us)
Async XLA Ops:
  7.2 91.2 %all-gather.4.cloned.1.call-start = ((), (), s32[]{:S(2)}) async-start(), calls=%async_computation.2 | async-start | bytes 2654208 | tf_op jit(solution)/shard_map/all_gather | solution.py:125
  7.9 130.6 %all-gather.6.cloned.1.call-start = ((), (), s32[]{:S(2)}) async-start(), calls=%async_computation.3 | async-start | bytes 2654208 | tf_op jit(solution)/shard_map/all_gather | solution.py:127
  8.9 42.8 %collective-permute-start = (bf16[1,3,32,384]{3,2,1,0:T(8,128)(2,1)S(1)}, bf16[1,3,32,384]{3,2,1,0:T(8,128)(2,1)S(1)}, u32[]{:S(2)}, u32[]{:S(2)}) collective-permute-start(bf16[1,3,32,384]{3,2,1,0:T(8,128)(2,1)S(1)} %get-tuple-element.210), channel_id=1, source_target_pairs={{0,8},{8,16},{16,24},{1,9},{9,17},{17,25},{2,10},{10,18},{18,26},{... | collective-permute-start | bytes 221192 | tf_op jit(solution)/shard_map/ppermute | solution.py:19
  13.5 38.6 %collective-permute-start.1 = (bf16[1,3,32,384]{3,2,1,0:T(8,128)(2,1)S(1)}, bf16[1,3,32,384]{3,2,1,0:T(8,128)(2,1)S(1)}, u32[]{:S(2)}, u32[]{:S(2)}) collective-permute-start(bf16[1,3,32,384]{3,2,1,0:T(8,128)(2,1)S(1)} %get-tuple-element.209), channel_id=1, source_target_pairs={{8,0},{16,8},{24,16},{9,1},{17,9},{25,17},{10,2},{18,10},{26,18},{... | collective-permute-start | bytes 221192 | tf_op jit(solution)/shard_map/ppermute | solution.py:20
  16.4 40.7 %collective-permute-start.4 = (bf16[1,3,32,384]{3,2,1,0:T(8,128)(2,1)S(1)}, bf16[1,3,32,384]{3,2,1,0:T(8,128)(2,1)S(1)}, u32[]{:S(2)}, u32[]{:S(2)}) collective-permute-start(bf16[1,3,32,384]{3,2,1,0:T(8,128)(2,1)S(1)} %get-tuple-element.205), channel_id=1, source_target_pairs={{0,8},{8,16},{16,24},{1,9},{9,17},{17,25},{2,10},{10,18},{18,26},{... | collective-permute-start | bytes 221192 | tf_op jit(solution)/shard_map/ppermute | solution.py:19
  20.0 37.5 %collective-permute-start.5 = (bf16[1,3,32,384]{3,2,1,0:T(8,128)(2,1)S(1)}, bf16[1,3,32,384]{3,2,1,0:T(8,128)(2,1)S(1)}, u32[]{:S(2)}, u32[]{:S(2)}) collective-permute-start(bf16[1,3,32,384]{3,2,1,0:T(8,128)(2,1)S(1)} %get-tuple-element.204), channel_id=1, source_target_pairs={{8,0},{16,8},{24,16},{9,1},{17,9},{25,17},{10,2},{18,10},{26,18},{... | collective-permute-start | bytes 221192 | tf_op jit(solution)/shard_map/ppermute | solution.py:20
  22.0 398.7 %all-reduce.6.cloned.1.call-start = ((), (), s32[]{:S(2)}) async-start(), calls=%async_computation.6 | async-start | bytes 172032 | tf_op jit(solution)/shard_map/psum | solution.py:156
  25.9 53.8 %copy-start.19 = (f32[384]{0:T(512)}, f32[384]{0:T(512)S(1)}, u32[]{:S(2)}) copy-start(f32[384]{0:T(512)S(1)} %get-tuple-element.90) | copy-start | bytes 4612
  25.9 53.8 %copy-start.20 = (f32[384]{0:T(512)}, f32[384]{0:T(512)S(1)}, u32[]{:S(2)}) copy-start(f32[384]{0:T(512)S(1)} %get-tuple-element.91) | copy-start | bytes 4612
  25.9 53.8 %copy-start.21 = (f32[384]{0:T(512)}, f32[384]{0:T(512)S(1)}, u32[]{:S(2)}) copy-start(f32[384]{0:T(512)S(1)} %get-tuple-element.92) | copy-start | bytes 4612
  25.9 53.8 %copy-start.22 = (f32[384]{0:T(512)}, f32[384]{0:T(512)S(1)}, u32[]{:S(2)}) copy-start(f32[384]{0:T(512)S(1)} %get-tuple-element.93) | copy-start | bytes 4612
  25.9 53.8 %copy-start.23 = (f32[384]{0:T(512)}, f32[384]{0:T(512)S(1)}, u32[]{:S(2)}) copy-start(f32[384]{0:T(512)S(1)} %get-tuple-element.94) | copy-start | bytes 4612
  25.9 53.8 %copy-start.24 = (f32[384]{0:T(512)}, f32[384]{0:T(512)S(1)}, u32[]{:S(2)}) copy-start(f32[384]{0:T(512)S(1)} %get-tuple-element.95) | copy-start | bytes 4612
  25.9 53.8 %copy-start.25 = (f32[384]{0:T(512)}, f32[384]{0:T(512)S(1)}, u32[]{:S(2)}) copy-start(f32[384]{0:T(512)S(1)} %get-tuple-element.96) | copy-start | bytes 4612
  25.9 53.8 %copy-start.26 = (f32[384]{0:T(512)}, f32[384]{0:T(512)S(1)}, u32[]{:S(2)}) copy-start(f32[384]{0:T(512)S(1)} %get-tuple-element.97) | copy-start | bytes 4612
  25.9 53.8 %copy-start.27 = (f32[384]{0:T(512)}, f32[384]{0:T(512)S(1)}, u32[]{:S(2)}) copy-start(f32[384]{0:T(512)S(1)} %get-tuple-element.98) | copy-start | bytes 4612
  25.9 53.8 %copy-start.28 = (f32[384]{0:T(512)}, f32[384]{0:T(512)S(1)}, u32[]{:S(2)}) copy-start(f32[384]{0:T(512)S(1)} %get-tuple-element.99) | copy-start | bytes 4612
  26.0 53.8 %copy-start.29 = (f32[384]{0:T(512)}, f32[384]{0:T(512)S(1)}, u32[]{:S(2)}) copy-start(f32[384]{0:T(512)S(1)} %get-tuple-element.100) | copy-start | bytes 4612
  26.0 53.8 %copy-start.30 = (f32[384]{0:T(512)}, f32[384]{0:T(512)S(1)}, u32[]{:S(2)}) copy-start(f32[384]{0:T(512)S(1)} %get-tuple-element.101) | copy-start | bytes 4612
  26.0 53.8 %copy-start.31 = (f32[384]{0:T(512)}, f32[384]{0:T(512)S(1)}, u32[]{:S(2)}) copy-start(f32[384]{0:T(512)S(1)} %get-tuple-element.102) | copy-start | bytes 4612
  26.0 53.8 %copy-start.32 = (f32[384]{0:T(512)}, f32[384]{0:T(512)S(1)}, u32[]{:S(2)}) copy-start(f32[384]{0:T(512)S(1)} %get-tuple-element.103) | copy-start | bytes 4612
  26.0 53.8 %copy-start.33 = (f32[384]{0:T(512)}, f32[384]{0:T(512)S(1)}, u32[]{:S(2)}) copy-start(f32[384]{0:T(512)S(1)} %get-tuple-element.104) | copy-start | bytes 4612
  26.0 53.8 %copy-start.34 = (f32[384]{0:T(512)}, f32[384]{0:T(512)S(1)}, u32[]{:S(2)}) copy-start(f32[384]{0:T(512)S(1)} %get-tuple-element.105) | copy-start | bytes 4612
  26.0 53.8 %copy-start.35 = (f32[384]{0:T(512)}, f32[384]{0:T(512)S(1)}, u32[]{:S(2)}) copy-start(f32[384]{0:T(512)S(1)} %get-tuple-element.106) | copy-start | bytes 4612
  26.0 53.8 %copy-start.36 = (f32[384]{0:T(512)}, f32[384]{0:T(512)S(1)}, u32[]{:S(2)}) copy-start(f32[384]{0:T(512)S(1)} %get-tuple-element.107) | copy-start | bytes 4612
  27.6 52.3 %copy-start.42 = (f32[384]{0:T(512)}, f32[384]{0:T(512)S(1)}, u32[]{:S(2)}) copy-start(f32[384]{0:T(512)S(1)} %get-tuple-element.75) | copy-start | bytes 4612
  27.6 52.3 %copy-start.43 = (f32[384]{0:T(512)}, f32[384]{0:T(512)S(1)}, u32[]{:S(2)}) copy-start(f32[384]{0:T(512)S(1)} %get-tuple-element.76) | copy-start | bytes 4612
  27.6 52.3 %copy-start.44 = (f32[384]{0:T(512)}, f32[384]{0:T(512)S(1)}, u32[]{:S(2)}) copy-start(f32[384]{0:T(512)S(1)} %get-tuple-element.77) | copy-start | bytes 4612
  27.6 52.3 %copy-start.45 = (f32[384]{0:T(512)}, f32[384]{0:T(512)S(1)}, u32[]{:S(2)}) copy-start(f32[384]{0:T(512)S(1)} %get-tuple-element.78) | copy-start | bytes 4612
  27.6 52.3 %copy-start.46 = (f32[384]{0:T(512)}, f32[384]{0:T(512)S(1)}, u32[]{:S(2)}) copy-start(f32[384]{0:T(512)S(1)} %get-tuple-element.79) | copy-start | bytes 4612
  27.6 52.3 %copy-start.47 = (f32[384]{0:T(512)}, f32[384]{0:T(512)S(1)}, u32[]{:S(2)}) copy-start(f32[384]{0:T(512)S(1)} %get-tuple-element.80) | copy-start | bytes 4612
  27.7 52.3 %copy-start.48 = (f32[384]{0:T(512)}, f32[384]{0:T(512)S(1)}, u32[]{:S(2)}) copy-start(f32[384]{0:T(512)S(1)} %get-tuple-element.81) | copy-start | bytes 4612
  27.7 52.3 %copy-start.49 = (f32[384]{0:T(512)}, f32[384]{0:T(512)S(1)}, u32[]{:S(2)}) copy-start(f32[384]{0:T(512)S(1)} %get-tuple-element.82) | copy-start | bytes 4612
  27.7 52.3 %copy-start.50 = (f32[384]{0:T(512)}, f32[384]{0:T(512)S(1)}, u32[]{:S(2)}) copy-start(f32[384]{0:T(512)S(1)} %get-tuple-element.83) | copy-start | bytes 4612
  52.3 11.2 %collective-permute-start.2 = (bf16[1,38,3,384]{3,2,1,0:T(4,128)(2,1)S(1)}, bf16[1,38,3,384]{3,2,1,0:T(4,128)(2,1)S(1)}, u32[]{:S(2)}, u32[]{:S(2)}) collective-permute-start(bf16[1,38,3,384]{3,2,1,0:T(4,128)(2,1)S(1)} %get-tuple-element.194), channel_id=1, source_target_pairs={{0,1},{1,2},{2,3},{3,4},{4,5},{5,6},{6,7},{8,9},{9,10},{10,11},{11... | collective-permute-start | bytes 262664 | tf_op jit(solution)/shard_map/ppermute | solution.py:19
  55.8 7.7 collective-permute-start.3
  57.7 21.9 %collective-permute-start.6 = (bf16[1,38,3,384]{3,2,1,0:T(4,128)(2,1)S(1)}, bf16[1,38,3,384]{3,2,1,0:T(4,128)(2,1)S(1)}, u32[]{:S(2)}, u32[]{:S(2)}) collective-permute-start(bf16[1,38,3,384]{3,2,1,0:T(4,128)(2,1)S(1)} %get-tuple-element.192), channel_id=1, source_target_pairs={{0,1},{1,2},{2,3},{3,4},{4,5},{5,6},{6,7},{8,9},{9,10},{10,11},{11... | collective-permute-start | bytes 262664 | tf_op jit(solution)/shard_map/ppermute | solution.py:19
  62.0 17.7 %collective-permute-start.7 = (bf16[1,38,3,384]{3,2,1,0:T(4,128)(2,1)S(1)}, bf16[1,38,3,384]{3,2,1,0:T(4,128)(2,1)S(1)}, u32[]{:S(2)}, u32[]{:S(2)}) collective-permute-start(bf16[1,38,3,384]{3,2,1,0:T(4,128)(2,1)S(1)} %get-tuple-element.193), channel_id=1, source_target_pairs={{1,0},{2,1},{3,2},{4,3},{5,4},{6,5},{7,6},{9,8},{10,9},{11,10},{12... | collective-permute-start | bytes 262664 | tf_op jit(solution)/shard_map/ppermute | solution.py:20
  175.5 326.6 %reduce-scatter.5.cloned.1.call-start = ((), (), s32[]{:S(2)}) async-start(), calls=%async_computation.5 | async-start | bytes 2654208 | tf_op jit(solution)/shard_map/reduce_scatter | solution.py:160
  180.7 407.1 %reduce-scatter.3.cloned.1.call-start = ((), (), s32[]{:S(2)}) async-start(), calls=%async_computation.4 | async-start | bytes 2654208 | tf_op jit(solution)/shard_map/reduce_scatter | solution.py:158
  187.0 632.0 %all-reduce.8.cloned.1.call-start = ((), (), s32[]{:S(2)}) async-start(), calls=%async_computation.7 | async-start | bytes 1179648 | tf_op jit(solution)/shard_map/psum | solution.py:162
  189.1 171.2 %collective-permute-start.8 = (bf16[1,3,32,384]{3,2,1,0:T(8,128)(2,1)S(1)}, bf16[1,3,32,384]{3,2,1,0:T(8,128)(2,1)S(1)}, u32[]{:S(2)}, u32[]{:S(2)}) collective-permute-start(bf16[1,3,32,384]{3,2,1,0:T(8,128)(2,1)S(1)} %get-tuple-element.199), channel_id=1, source_target_pairs={{0,8},{8,16},{16,24},{1,9},{9,17},{17,25},{2,10},{10,18},{18,26},{... | collective-permute-start | bytes 221192 | tf_op jit(solution)/shard_map/ppermute | solution.py:19
  193.4 157.2 %copy-start.13 = (bf16[1,32,32,384]{3,2,1,0:T(8,128)(2,1)S(1)}, bf16[1,32,32,384]{3,2,1,0:T(8,128)(2,1)}, u32[]{:S(2)}) copy-start(bf16[1,32,32,384]{3,2,1,0:T(8,128)(2,1)} %get-tuple-element.224) | copy-start | bytes 2359300
  193.5 157.2 %copy-start.57 = (f32[1536]{0:T(1024)S(1)}, f32[1536]{0:T(1024)}, u32[]{:S(2)}) copy-start(f32[1536]{0:T(1024)} %get-tuple-element.169) | copy-start | bytes 18436
  193.5 157.2 %copy-start.59 = (f32[384]{0:T(512)S(1)}, f32[384]{0:T(512)}, u32[]{:S(2)}) copy-start(f32[384]{0:T(512)} %get-tuple-element.172) | copy-start | bytes 4612
  193.5 166.9 %collective-permute-start.9 = (bf16[1,3,32,384]{3,2,1,0:T(8,128)(2,1)S(1)}, bf16[1,3,32,384]{3,2,1,0:T(8,128)(2,1)S(1)}, u32[]{:S(2)}, u32[]{:S(2)}) collective-permute-start(bf16[1,3,32,384]{3,2,1,0:T(8,128)(2,1)S(1)} %get-tuple-element.200), channel_id=1, source_target_pairs={{8,0},{16,8},{24,16},{9,1},{17,9},{25,17},{10,2},{18,10},{26,18},{... | collective-permute-start | bytes 221192 | tf_op jit(solution)/shard_map/ppermute | solution.py:20
  360.5 61.8 %collective-permute-start.10 = (bf16[1,38,3,384]{3,2,1,0:T(4,128)(2,1)S(1)}, bf16[1,38,3,384]{3,2,1,0:T(4,128)(2,1)S(1)}, u32[]{:S(2)}, u32[]{:S(2)}) collective-permute-start(bf16[1,38,3,384]{3,2,1,0:T(4,128)(2,1)S(1)} %get-tuple-element.190), channel_id=1, source_target_pairs={{0,1},{1,2},{2,3},{3,4},{4,5},{5,6},{6,7},{8,9},{9,10},{10,11},{11... | collective-permute-start | bytes 262664 | tf_op jit(solution)/shard_map/ppermute | solution.py:19
  362.8 59.5 %collective-permute-start.11 = (bf16[1,38,3,384]{3,2,1,0:T(4,128)(2,1)S(1)}, bf16[1,38,3,384]{3,2,1,0:T(4,128)(2,1)S(1)}, u32[]{:S(2)}, u32[]{:S(2)}) collective-permute-start(bf16[1,38,3,384]{3,2,1,0:T(4,128)(2,1)S(1)} %get-tuple-element.191), channel_id=1, source_target_pairs={{1,0},{2,1},{3,2},{4,3},{5,4},{6,5},{7,6},{9,8},{10,9},{11,10},{12... | collective-permute-start | bytes 262664 | tf_op jit(solution)/shard_map/ppermute | solution.py:20
  (35 other events, 782.8 us)
Sparse Core Ops, SparseCore 0:
  10.6 64.3 all-gather.3
  77.6 60.8 all-gather.5
  175.6 245.0 all-reduce.5
  424.7 77.4 reduce-scatter.4
  506.1 81.7 reduce-scatter.2
  590.4 228.6 all-reduce.7
where the time goes:
time: 831 us; the launch traced here: 829 us
  waiting for transfers between devices  470 us (57%)
  blocking collectives  171 us (21%)
  other arithmetic  92.2 us (11%)
  matrix products  34.8 us (4%)
  starting transfers between devices  32.8 us (4%)
  between operations  16.4 us (2%)
  local copies, waits for them, and re-layouts  12.1 us (1%)
    psum x1, waiting for transfers between devices, on_device(): shares = lax.psum((owned[0], owned[1], owned[2]), ('row', 'col'))  214 us
    reduce_scatter x1, waiting for transfers between devices, on_device(): lax.psum_scatter(large_grads[0], 'dp', scatter_dimension=1, tiled=True)  85.7 us
    reduce_scatter x1, waiting for transfers between devices, on_device(): lax.psum_scatter(large_grads[2], 'dp', scatter_dimension=0, tiled=True)  79.1 us
    psum x1, blocking collectives, on_device(): lax.psum((minor_grads[0], minor_grads[1], minor_grads[2]), ('dp', 'row',...  77.7 us
    psum x1, waiting for transfers between devices, on_device(): lax.psum((minor_grads[0], minor_grads[1], minor_grads[2]), ('dp', 'row',...  56.6 us
    psum x1, blocking collectives, on_device(): shares = lax.psum((owned[0], owned[1], owned[2]), ('row', 'col'))  54.5 us
    all_gather x1, waiting for transfers between devices, on_device(): lax.all_gather(weight_out, 'dp', axis=1, tiled=True)  33.4 us
    reduce_sum x2, other arithmetic, forward(): centered = convolved - jnp.mean(convolved, axis=-1, keepdims=True)  32.2 us
  transfers between devices with their start and end apart: 18, of which 5 were waited for; matrix products, arithmetic and copies ran while one was open for 12% of the time, Pallas kernels for 0%

commit v1 on v0

--- a/solution.py
+++ b/solution.py
@@ -159,7 +159,7 @@
         lax.psum_scatter(large_grads[1], "dp", scatter_dimension=0, tiled=True),
         lax.psum_scatter(large_grads[2], "dp", scatter_dimension=0, tiled=True),
     )
-    shares = lax.psum((owned[0], owned[1], owned[2]), ("row", "col"))
+    shares = lax.psum(lax.psum((owned[0], owned[1], owned[2]), "row"), "col")
     tokens = (
         teacher_in.shape[0]
         * teacher_in.shape[1]

time: 831 us -> 697 us (0.84)
  waiting for transfers between devices: 470 us -> 368 us
  blocking collectives: 171 us -> 136 us
    psum x1, waiting for transfers between devices: 56.6 us -> 238 us  [on_device(): lax.psum((minor_grads[0], minor_grads[1], minor_grads[2]), ('dp', 'row',...]
    psum x1 -> x2, waiting for transfers between devices: 214 us -> 94.7 us  [on_device(): shares = lax.psum(lax.psum((owned[0], owned[1], owned[2]), 'row'), 'col')]
    reduce_scatter x1, waiting for transfers between devices: 85.7 us -> 0.02 us  [on_device(): lax.psum_scatter(large_grads[0], 'dp', scatter_dimension=1, tiled=True)]
    reduce_scatter x1, waiting for transfers between devices: 79.1 us -> 0.01 us  [on_device(): lax.psum_scatter(large_grads[2], 'dp', scatter_dimension=0, tiled=True)]
    psum x1 -> x2, blocking collectives: 54.5 us -> 22.3 us  [on_device(): shares = lax.psum(lax.psum((owned[0], owned[1], owned[2]), 'row'), 'col')]
  transfers between devices with their start and end apart: 18 -> 19, of which waited for: 5 -> 4; matrix products, arithmetic and copies ran while one was open for 12% -> 18% of each run, Pallas kernels for 0% -> 0%
where the time goes in v1:
time: 697 us; the launch traced here: 692 us
  waiting for transfers between devices  368 us (53%)
  blocking collectives  136 us (20%)
  other arithmetic  91.3 us (13%)
  matrix products  34.6 us (5%)
  starting transfers between devices  32.1 us (5%)
  between operations  16.7 us (2%)
  local copies, waits for them, and re-layouts  13.1 us (2%)
    psum x1, waiting for transfers between devices, on_device(): lax.psum((minor_grads[0], minor_grads[1], minor_grads[2]), ('dp', 'row',...  238 us
    psum x2, waiting for transfers between devices, on_device(): shares = lax.psum(lax.psum((owned[0], owned[1], owned[2]), 'row'), 'col')  94.7 us
    psum x1, blocking collectives, on_device(): lax.psum((minor_grads[0], minor_grads[1], minor_grads[2]), ('dp', 'row',...  77 us
    all_gather x1, waiting for transfers between devices, on_device(): lax.all_gather(weight_out, 'dp', axis=1, tiled=True)  34.4 us
    reduce_sum x2, other arithmetic, forward(): centered = convolved - jnp.mean(convolved, axis=-1, keepdims=True)  31.6 us
    psum x2, blocking collectives, on_device(): shares = lax.psum(lax.psum((owned[0], owned[1], owned[2]), 'row'), 'col')  22.3 us
    ppermute x6, starting transfers between devices, with_halo(): before = lax.ppermute(last, axis, up)  21.5 us
    all_gather x1, blocking collectives, on_device(): lax.all_gather(bias_in, 'dp', axis=1, tiled=True)  19.7 us
  transfers between devices with their start and end apart: 19, of which 4 were waited for; matrix products, arithmetic and copies ran while one was open for 18% of the time, Pallas kernels for 0%

profile of v1, /device:TPU:1, one launch (start us, length us, event | category | flops | bytes accessed | tf_op | source)
XLA Modules:
  0.0 692.0 jit_solution(2500440113308345213)
XLA Ops:
  8.9 4.6 collective-permute-start
  13.5 1.9 collective-permute-start.1
  16.4 3.6 collective-permute-start.4
  20.0 1.9 collective-permute-start.5
  27.2 1.4 convert_reduce_fusion.3
  28.6 1.4 convert_reduce_fusion.56
  29.9 19.7 %all-gather = bf16[8,192,2]{1,2,0:T(2,128)(2,1)S(1)} all-gather(bf16[1,192,2]{1,2,0:T(2,128)(2,1)} %bitcast.59), channel_id=1, replica_groups=mesh['dp'=8,'row'=4,'col'=8] {'dp'}, dimensions={0}, use_global_device_ids=true | all-gather | bytes 6912 | tf_op jit(solution)/shard_map/all_gather | solution.py:126
  51.7 3.5 collective-permute-start.2
  55.2 1.3 collective-permute-start.3
  57.1 4.2 collective-permute-start.6
  61.4 1.5 collective-permute-start.7
  62.9 15.8 %fusion.250 = (f32[32,32]{1,0:T(8,128)S(1)}, f32[1,32,32,384]{3,2,1,0:T(8,128)S(1)}) fusion(f32[384]{0:T(512)S(1)} %get-tuple-element.174, f32[384]{0:T(512)S(1)} %get-tuple-element.117, bf16[1,38,3,384]{3,2,1,0:T(4,128)(2,1)S(1)} %collective-permute-done.3, bf16[1,38,32,384]{3,2,1,0:T(8,128)(2,1)S(1)} %get-tuple-element.220, ...), kind=kLoop, calls=%fused_computation.649 | loop fusion | flops 107740160 | bytes 8267776 | tf_op jit(solution)/shard_map/reduce_sum | solution.py:48
  79.4 15.8 %fusion.248 = (f32[32,32]{1,0:T(8,128)S(1)}, f32[1,32,32,384]{3,2,1,0:T(8,128)S(1)}) fusion(f32[384]{0:T(512)S(1)} %copy-done.81, f32[384]{0:T(512)S(1)} %get-tuple-element.146, bf16[1,38,3,384]{3,2,1,0:T(4,128)(2,1)S(1)} %collective-permute-done.7, bf16[1,38,32,384]{3,2,1,0:T(8,128)(2,1)S(1)} %get-tuple-element.216, f32[384]{0:T(512)S(1)} %get-tuple-element.127, ...), kind=kLoop, calls=%fused_computation.648 | loop fusion | flops 107740160 | bytes 8267776 | tf_op jit(solution)/shard_map/reduce_sum | solution.py:48
  95.9 1.5 add_convert_fusion
  97.4 6.7 multiply_convert_fusion
  104.1 34.4 %all-gather.6.cloned.1.call-done = bf16[2,1536,384]{2,1,0:T(8,128)(2,1)} async-done(((bf16[2,192,384]{2,1,0:T(8,128)(2,1)}), bf16[2,1536,384]{2,1,0:T(8,128)(2,1)}) %all-gather.6.cloned.1.call-update) | async-done | bytes 2359312 | tf_op jit(solution)/shard_map/all_gather | solution.py:127
  138.5 6.1 fusion.153
  144.7 3.3 fusion.258
  149.9 6.2 fusion.4
  156.1 3.5 fusion.247
  159.7 3.4 multiply_reduce_fusion
  163.9 1.1 copy-done.11
  165.2 3.3 fusion.257
  168.6 1.1 copy-done.1
  170.0 5.2 fusion.149
  175.5 2.7 fusion.146
  178.2 3.2 fusion.150
  181.6 2.7 fusion.147
  184.4 3.1 fusion.151
  188.2 4.1 collective-permute-start.8
  192.3 1.9 collective-permute-start.9
  194.3 4.4 stack.220
  198.6 77.0 %all-reduce.1 = (f32[2,384]{1,0:T(2,128)S(1)}, f32[3,384]{1,0:T(4,128)S(1)}) all-reduce(f32[2,384]{1,0:T(2,128)S(1)} %pad_maximum_fusion.11, f32[3,384]{1,0:T(4,128)S(1)} %pad_maximum_fusion.10), channel_id=1, replica_groups=mesh['dp'=8,'row'=4,'col'=8] {'dp','row','col'}, use_global_device_ids=true, to_apply=%region_68.0 | all-reduce | flops 1920 | bytes 15360 | tf_op jit(solution)/shard_map/psum | solution.py:156
  277.1 5.5 convolution_add_fusion.1
  282.7 1.4 convert_add_fusion.1
  285.6 17.5 %all-reduce = f32[1536]{0:T(1024)S(1)} all-reduce(f32[1536]{0:T(1024)S(1)} %convert_reduce_fusion.1), channel_id=3, replica_groups=mesh['dp'=8,'row'=4,'col'=8] {'dp'}, use_global_device_ids=true, to_apply=%region_10.0.clone | all-reduce | flops 1536 | bytes 12288
  303.2 9.5 %psum.65 = f32[192]{0:T(256)S(1)} all-reduce(f32[192]{0:T(256)S(1)} %dynamic-slice.1), channel_id=1, replica_groups=mesh['dp'=8,'row'=4,'col'=8] {'row'}, use_global_device_ids=true, to_apply=%region_11.0 | all-reduce | flops 192 | bytes 1536 | tf_op jit(solution)/shard_map/psum | solution.py:162
  312.7 12.8 %psum.66 = f32[192]{0:T(256)S(1)} all-reduce(f32[192]{0:T(256)S(1)} %psum.65), channel_id=1, replica_groups=mesh['dp'=8,'row'=4,'col'=8] {'col'}, use_global_device_ids=true, to_apply=%region_12.0 | all-reduce | flops 192 | bytes 1536 | tf_op jit(solution)/shard_map/psum | solution.py:162
  326.3 1.4 collective-permute-start.10
  327.7 1.3 collective-permute-start.11
  329.0 237.8 %all-reduce.8.cloned.1.call-done = f32[49,384]{1,0:T(8,128)} async-done(((f32[49,384]{1,0:T(8,128)}), f32[49,384]{1,0:T(8,128)}) %all-reduce.8.cloned.1.call-update) | async-done | bytes 75280 | tf_op jit(solution)/shard_map/psum | solution.py:156
  566.8 1.5 broadcast_multiply_fusion.2
  568.6 1.6 maximum_maximum_fusion
  570.2 39.2 %all-reduce.12.cloned.1.call-done = (f32[384,192]{0,1:T(8,128)}, f32[192,384]{1,0:T(8,128)}) async-done(((f32[384,192]{0,1:T(8,128)}, f32[192,384]{1,0:T(8,128)}), (f32[384,192]{0,1:T(8,128)}, f32[192,384]{1,0:T(8,128)})) %all-reduce.12.cloned.1.call-update) | async-done | bytes 589840 | tf_op jit(solution)/shard_map/psum | solution.py:162
  609.6 16.6 %convert_add_fusion.2 = f32[1,32,32,384]{3,2,1,0:T(8,128)} fusion(bf16[1,32,32,384]{3,2,1,0:T(8,128)(2,1)} %param.11, bf16[1,32,32,384]{3,2,1,0:T(8,128)(2,1)S(1)} %multiply_convert_fusion.2, bf16[1,3,32,384]{3,2,1,0:T(8,128)(2,1)S(1)} %collective-permute-done.9, bf16[1,3,32,384]{3,2,1,0:T(8,128)(2,1)S(1)} %collective-permute-done.8, ...), kind=kLoop, calls=%fused_computation.342 | loop fusion | flops 60555264 | bytes 36398592 | tf_op jit(solution)/shard_map/add | solution.py:117
  626.3 55.5 %all-reduce.10.cloned.1.call-done = (f32[384,192]{0,1:T(8,128)}, f32[192,384]{1,0:T(8,128)}) async-done(((f32[384,192]{0,1:T(8,128)}, f32[192,384]{1,0:T(8,128)}), (f32[384,192]{0,1:T(8,128)}, f32[192,384]{1,0:T(8,128)})) %all-reduce.10.cloned.1.call-update) | async-done | bytes 589840 | tf_op jit(solution)/shard_map/psum | solution.py:162
  681.8 1.7 broadcast_multiply_fusion
  683.5 1.7 broadcast_multiply_fusion.1
  (302 shorter events, 18.7 us)
Async XLA Ops:
  7.2 90.2 %all-gather.4.cloned.1.call-start = ((), (), s32[]{:S(2)}) async-start(), calls=%async_computation.2 | async-start | bytes 2654208 | tf_op jit(solution)/shard_map/all_gather | solution.py:125
  7.9 130.6 %all-gather.6.cloned.1.call-start = ((), (), s32[]{:S(2)}) async-start(), calls=%async_computation.3 | async-start | bytes 2654208 | tf_op jit(solution)/shard_map/all_gather | solution.py:127
  8.9 42.2 %collective-permute-start = (bf16[1,3,32,384]{3,2,1,0:T(8,128)(2,1)S(1)}, bf16[1,3,32,384]{3,2,1,0:T(8,128)(2,1)S(1)}, u32[]{:S(2)}, u32[]{:S(2)}) collective-permute-start(bf16[1,3,32,384]{3,2,1,0:T(8,128)(2,1)S(1)} %get-tuple-element.212), channel_id=1, source_target_pairs={{0,8},{8,16},{16,24},{1,9},{9,17},{17,25},{2,10},{10,18},{18,26},{... | collective-permute-start | bytes 221192 | tf_op jit(solution)/shard_map/ppermute | solution.py:19
  13.5 38.0 %collective-permute-start.1 = (bf16[1,3,32,384]{3,2,1,0:T(8,128)(2,1)S(1)}, bf16[1,3,32,384]{3,2,1,0:T(8,128)(2,1)S(1)}, u32[]{:S(2)}, u32[]{:S(2)}) collective-permute-start(bf16[1,3,32,384]{3,2,1,0:T(8,128)(2,1)S(1)} %get-tuple-element.211), channel_id=1, source_target_pairs={{8,0},{16,8},{24,16},{9,1},{17,9},{25,17},{10,2},{18,10},{26,18},{... | collective-permute-start | bytes 221192 | tf_op jit(solution)/shard_map/ppermute | solution.py:20
  16.4 40.1 %collective-permute-start.4 = (bf16[1,3,32,384]{3,2,1,0:T(8,128)(2,1)S(1)}, bf16[1,3,32,384]{3,2,1,0:T(8,128)(2,1)S(1)}, u32[]{:S(2)}, u32[]{:S(2)}) collective-permute-start(bf16[1,3,32,384]{3,2,1,0:T(8,128)(2,1)S(1)} %get-tuple-element.207), channel_id=1, source_target_pairs={{0,8},{8,16},{16,24},{1,9},{9,17},{17,25},{2,10},{10,18},{18,26},{... | collective-permute-start | bytes 221192 | tf_op jit(solution)/shard_map/ppermute | solution.py:19
  20.0 36.9 %collective-permute-start.5 = (bf16[1,3,32,384]{3,2,1,0:T(8,128)(2,1)S(1)}, bf16[1,3,32,384]{3,2,1,0:T(8,128)(2,1)S(1)}, u32[]{:S(2)}, u32[]{:S(2)}) collective-permute-start(bf16[1,3,32,384]{3,2,1,0:T(8,128)(2,1)S(1)} %get-tuple-element.206), channel_id=1, source_target_pairs={{8,0},{16,8},{24,16},{9,1},{17,9},{25,17},{10,2},{18,10},{26,18},{... | collective-permute-start | bytes 221192 | tf_op jit(solution)/shard_map/ppermute | solution.py:20
  22.0 303.6 %reduce-scatter.5.cloned.1.call-start = ((), (), s32[]{:S(2)}) async-start(), calls=%async_computation.5 | async-start | bytes 2654208 | tf_op jit(solution)/shard_map/reduce_scatter | solution.py:160
  25.9 53.2 %copy-start.19 = (f32[384]{0:T(512)}, f32[384]{0:T(512)S(1)}, u32[]{:S(2)}) copy-start(f32[384]{0:T(512)S(1)} %get-tuple-element.95) | copy-start | bytes 4612
  25.9 53.2 %copy-start.21 = (f32[384]{0:T(512)}, f32[384]{0:T(512)S(1)}, u32[]{:S(2)}) copy-start(f32[384]{0:T(512)S(1)} %get-tuple-element.96) | copy-start | bytes 4612
  25.9 53.2 %copy-start.23 = (f32[384]{0:T(512)}, f32[384]{0:T(512)S(1)}, u32[]{:S(2)}) copy-start(f32[384]{0:T(512)S(1)} %get-tuple-element.97) | copy-start | bytes 4612
  25.9 53.2 %copy-start.25 = (f32[384]{0:T(512)}, f32[384]{0:T(512)S(1)}, u32[]{:S(2)}) copy-start(f32[384]{0:T(512)S(1)} %get-tuple-element.98) | copy-start | bytes 4612
  25.9 53.2 %copy-start.27 = (f32[384]{0:T(512)}, f32[384]{0:T(512)S(1)}, u32[]{:S(2)}) copy-start(f32[384]{0:T(512)S(1)} %get-tuple-element.99) | copy-start | bytes 4612
  25.9 53.2 %copy-start.29 = (f32[384]{0:T(512)}, f32[384]{0:T(512)S(1)}, u32[]{:S(2)}) copy-start(f32[384]{0:T(512)S(1)} %get-tuple-element.100) | copy-start | bytes 4612
  25.9 53.2 %copy-start.31 = (f32[384]{0:T(512)}, f32[384]{0:T(512)S(1)}, u32[]{:S(2)}) copy-start(f32[384]{0:T(512)S(1)} %get-tuple-element.101) | copy-start | bytes 4612
  25.9 53.2 %copy-start.33 = (f32[384]{0:T(512)}, f32[384]{0:T(512)S(1)}, u32[]{:S(2)}) copy-start(f32[384]{0:T(512)S(1)} %get-tuple-element.102) | copy-start | bytes 4612
  25.9 53.2 %copy-start.35 = (f32[384]{0:T(512)}, f32[384]{0:T(512)S(1)}, u32[]{:S(2)}) copy-start(f32[384]{0:T(512)S(1)} %get-tuple-element.103) | copy-start | bytes 4612
  25.9 53.2 %copy-start.37 = (f32[384]{0:T(512)}, f32[384]{0:T(512)S(1)}, u32[]{:S(2)}) copy-start(f32[384]{0:T(512)S(1)} %get-tuple-element.104) | copy-start | bytes 4612
  26.0 53.2 %copy-start.39 = (f32[384]{0:T(512)}, f32[384]{0:T(512)S(1)}, u32[]{:S(2)}) copy-start(f32[384]{0:T(512)S(1)} %get-tuple-element.105) | copy-start | bytes 4612
  26.0 53.2 %copy-start.41 = (f32[384]{0:T(512)}, f32[384]{0:T(512)S(1)}, u32[]{:S(2)}) copy-start(f32[384]{0:T(512)S(1)} %get-tuple-element.106) | copy-start | bytes 4612
  26.0 53.2 %copy-start.43 = (f32[384]{0:T(512)}, f32[384]{0:T(512)S(1)}, u32[]{:S(2)}) copy-start(f32[384]{0:T(512)S(1)} %get-tuple-element.107) | copy-start | bytes 4612
  27.0 52.2 %copy-start.45 = (f32[384]{0:T(512)}, f32[384]{0:T(512)S(1)}, u32[]{:S(2)}) copy-start(f32[384]{0:T(512)S(1)} %get-tuple-element.70) | copy-start | bytes 4612
  27.0 52.2 %copy-start.47 = (f32[384]{0:T(512)}, f32[384]{0:T(512)S(1)}, u32[]{:S(2)}) copy-start(f32[384]{0:T(512)S(1)} %get-tuple-element.71) | copy-start | bytes 4612
  27.0 52.2 %copy-start.49 = (f32[384]{0:T(512)}, f32[384]{0:T(512)S(1)}, u32[]{:S(2)}) copy-start(f32[384]{0:T(512)S(1)} %get-tuple-element.72) | copy-start | bytes 4612
  27.0 52.2 %copy-start.51 = (f32[384]{0:T(512)}, f32[384]{0:T(512)S(1)}, u32[]{:S(2)}) copy-start(f32[384]{0:T(512)S(1)} %get-tuple-element.73) | copy-start | bytes 4612
  27.0 52.2 %copy-start.53 = (f32[384]{0:T(512)}, f32[384]{0:T(512)S(1)}, u32[]{:S(2)}) copy-start(f32[384]{0:T(512)S(1)} %get-tuple-element.74) | copy-start | bytes 4612
  27.0 52.2 %copy-start.55 = (f32[384]{0:T(512)}, f32[384]{0:T(512)S(1)}, u32[]{:S(2)}) copy-start(f32[384]{0:T(512)S(1)} %get-tuple-element.75) | copy-start | bytes 4612
  27.0 52.2 %copy-start.57 = (f32[384]{0:T(512)}, f32[384]{0:T(512)S(1)}, u32[]{:S(2)}) copy-start(f32[384]{0:T(512)S(1)} %get-tuple-element.76) | copy-start | bytes 4612
  27.0 52.2 %copy-start.59 = (f32[384]{0:T(512)}, f32[384]{0:T(512)S(1)}, u32[]{:S(2)}) copy-start(f32[384]{0:T(512)S(1)} %get-tuple-element.77) | copy-start | bytes 4612
  27.1 52.2 %copy-start.61 = (f32[384]{0:T(512)}, f32[384]{0:T(512)S(1)}, u32[]{:S(2)}) copy-start(f32[384]{0:T(512)S(1)} %get-tuple-element.78) | copy-start | bytes 4612
  27.1 52.2 %copy-start.63 = (f32[384]{0:T(512)}, f32[384]{0:T(512)S(1)}, u32[]{:S(2)}) copy-start(f32[384]{0:T(512)S(1)} %get-tuple-element.79) | copy-start | bytes 4612
  27.1 52.2 %copy-start.65 = (f32[384]{0:T(512)}, f32[384]{0:T(512)S(1)}, u32[]{:S(2)}) copy-start(f32[384]{0:T(512)S(1)} %get-tuple-element.80) | copy-start | bytes 4612
  27.1 52.2 %copy-start.67 = (f32[384]{0:T(512)}, f32[384]{0:T(512)S(1)}, u32[]{:S(2)}) copy-start(f32[384]{0:T(512)S(1)} %get-tuple-element.81) | copy-start | bytes 4612
  27.1 52.2 %copy-start.68 = (f32[384]{0:T(512)}, f32[384]{0:T(512)S(1)}, u32[]{:S(2)}) copy-start(f32[384]{0:T(512)S(1)} %get-tuple-element.82) | copy-start | bytes 4612
  27.1 52.2 %copy-start.69 = (f32[384]{0:T(512)}, f32[384]{0:T(512)S(1)}, u32[]{:S(2)}) copy-start(f32[384]{0:T(512)S(1)} %get-tuple-element.83) | copy-start | bytes 4612
  29.9 108.6 %copy-start.76 = (f32[384]{0:T(512)}, f32[384]{0:T(512)S(1)}, u32[]{:S(2)}) copy-start(f32[384]{0:T(512)S(1)} %get-tuple-element.176) | copy-start | bytes 4612
  51.7 11.2 %collective-permute-start.2 = (bf16[1,38,3,384]{3,2,1,0:T(4,128)(2,1)S(1)}, bf16[1,38,3,384]{3,2,1,0:T(4,128)(2,1)S(1)}, u32[]{:S(2)}, u32[]{:S(2)}) collective-permute-start(bf16[1,38,3,384]{3,2,1,0:T(4,128)(2,1)S(1)} %get-tuple-element.196), channel_id=1, source_target_pairs={{0,1},{1,2},{2,3},{3,4},{4,5},{5,6},{6,7},{8,9},{9,10},{10,11},{11... | collective-permute-start | bytes 262664 | tf_op jit(solution)/shard_map/ppermute | solution.py:19
  55.2 7.7 %collective-permute-start.3 = (bf16[1,38,3,384]{3,2,1,0:T(4,128)(2,1)S(1)}, bf16[1,38,3,384]{3,2,1,0:T(4,128)(2,1)S(1)}, u32[]{:S(2)}, u32[]{:S(2)}) collective-permute-start(bf16[1,38,3,384]{3,2,1,0:T(4,128)(2,1)S(1)} %get-tuple-element.197), channel_id=1, source_target_pairs={{1,0},{2,1},{3,2},{4,3},{5,4},{6,5},{7,6},{9,8},{10,9},{11,10},{12... | collective-permute-start | bytes 262664 | tf_op jit(solution)/shard_map/ppermute | solution.py:20
  57.1 21.9 %collective-permute-start.6 = (bf16[1,38,3,384]{3,2,1,0:T(4,128)(2,1)S(1)}, bf16[1,38,3,384]{3,2,1,0:T(4,128)(2,1)S(1)}, u32[]{:S(2)}, u32[]{:S(2)}) collective-permute-start(bf16[1,38,3,384]{3,2,1,0:T(4,128)(2,1)S(1)} %get-tuple-element.194), channel_id=1, source_target_pairs={{0,1},{1,2},{2,3},{3,4},{4,5},{5,6},{6,7},{8,9},{9,10},{10,11},{11... | collective-permute-start | bytes 262664 | tf_op jit(solution)/shard_map/ppermute | solution.py:19
  61.4 17.7 %collective-permute-start.7 = (bf16[1,38,3,384]{3,2,1,0:T(4,128)(2,1)S(1)}, bf16[1,38,3,384]{3,2,1,0:T(4,128)(2,1)S(1)}, u32[]{:S(2)}, u32[]{:S(2)}) collective-permute-start(bf16[1,38,3,384]{3,2,1,0:T(4,128)(2,1)S(1)} %get-tuple-element.195), channel_id=1, source_target_pairs={{1,0},{2,1},{3,2},{4,3},{5,4},{6,5},{7,6},{9,8},{10,9},{11,10},{12... | collective-permute-start | bytes 262664 | tf_op jit(solution)/shard_map/ppermute | solution.py:20
  148.0 177.6 %reduce-scatter.3.cloned.1.call-start = ((), (), s32[]{:S(2)}) async-start(), calls=%async_computation.4 | async-start | bytes 2654208 | tf_op jit(solution)/shard_map/reduce_scatter | solution.py:158
  168.5 398.3 %all-reduce.8.cloned.1.call-start = ((), (), s32[]{:S(2)}) async-start(), calls=%async_computation.6 | async-start | bytes 172032 | tf_op jit(solution)/shard_map/psum | solution.py:156
  187.6 89.5 %copy-start.82 = (f32[1536]{0:T(1024)S(1)}, f32[1536]{0:T(1024)}, u32[]{:S(2)}) copy-start(f32[1536]{0:T(1024)} %get-tuple-element.169) | copy-start | bytes 18436
  188.2 138.0 %collective-permute-start.8 = (bf16[1,3,32,384]{3,2,1,0:T(8,128)(2,1)S(1)}, bf16[1,3,32,384]{3,2,1,0:T(8,128)(2,1)S(1)}, u32[]{:S(2)}, u32[]{:S(2)}) collective-permute-start(bf16[1,3,32,384]{3,2,1,0:T(8,128)(2,1)S(1)} %get-tuple-element.201), channel_id=1, source_target_pairs={{0,8},{8,16},{16,24},{1,9},{9,17},{17,25},{2,10},{10,18},{18,26},{... | collective-permute-start | bytes 221192 | tf_op jit(solution)/shard_map/ppermute | solution.py:19
  192.3 133.9 %collective-permute-start.9 = (bf16[1,3,32,384]{3,2,1,0:T(8,128)(2,1)S(1)}, bf16[1,3,32,384]{3,2,1,0:T(8,128)(2,1)S(1)}, u32[]{:S(2)}, u32[]{:S(2)}) collective-permute-start(bf16[1,3,32,384]{3,2,1,0:T(8,128)(2,1)S(1)} %get-tuple-element.202), channel_id=1, source_target_pairs={{8,0},{16,8},{24,16},{9,1},{17,9},{25,17},{10,2},{18,10},{26,18},{... | collective-permute-start | bytes 221192 | tf_op jit(solution)/shard_map/ppermute | solution.py:20
  276.8 332.6 %all-reduce.12.cloned.1.call-start = ((), (), s32[]{:S(2)}) async-start(), calls=%async_computation.8 | async-start | bytes 1179648 | tf_op jit(solution)/shard_map/psum | solution.py:162
  325.6 356.2 %all-reduce.10.cloned.1.call-start = ((), (), s32[]{:S(2)}) async-start(), calls=%async_computation.7 | async-start | bytes 1179648 | tf_op jit(solution)/shard_map/psum | solution.py:162
  326.3 242.2 %collective-permute-start.10 = (bf16[1,38,3,384]{3,2,1,0:T(4,128)(2,1)S(1)}, bf16[1,38,3,384]{3,2,1,0:T(4,128)(2,1)S(1)}, u32[]{:S(2)}, u32[]{:S(2)}) collective-permute-start(bf16[1,38,3,384]{3,2,1,0:T(4,128)(2,1)S(1)} %get-tuple-element.192), channel_id=1, source_target_pairs={{0,1},{1,2},{2,3},{3,4},{4,5},{5,6},{6,7},{8,9},{9,10},{10,11},{11... | collective-permute-start | bytes 262664 | tf_op jit(solution)/shard_map/ppermute | solution.py:19
  327.7 240.8 %collective-permute-start.11 = (bf16[1,38,3,384]{3,2,1,0:T(4,128)(2,1)S(1)}, bf16[1,38,3,384]{3,2,1,0:T(4,128)(2,1)}, u32[]{:S(2)}, u32[]{:S(2)}) collective-permute-start(bf16[1,38,3,384]{3,2,1,0:T(4,128)(2,1)S(1)} %get-tuple-element.193), channel_id=1, source_target_pairs={{1,0},{2,1},{3,2},{4,3},{5,4},{6,5},{7,6},{9,8},{10,9},{11,10},{12... | collective-permute-start | bytes 262664 | tf_op jit(solution)/shard_map/ppermute | solution.py:20
  (61 other events, 1510.7 us)
Sparse Core Ops, SparseCore 0:
  10.6 64.3 all-gather.3
  77.6 60.8 all-gather.5
  148.1 81.8 reduce-scatter.4
  233.9 81.9 reduce-scatter.2
  321.8 244.9 all-reduce.7
  569.3 39.9 all-reduce.11
  611.8 69.9 all-reduce.9
